TPU v7x, 256 devices: a whole 4x4x8 slice. The times are simulated.
256 devices in a mesh: seq: 64 (over z, y, x_hi), tp: 4 (over x_lo, core).
Axes of the slice: x: 4 (x_hi: 2, x_lo: 2; x = x_hi * 2 + x_lo), y: 4, z: 8, core: 2. Of those that a mesh axis runs over, the one named last changes fastest.
Arguments:
- latents: bfloat16 [16384, 5120], P('seq', 'tp'), may hold values from -6 to 6
- noise: bfloat16 [16384, 5120], P('seq', 'tp'), may hold values from -6 to 6
- tstep: int32 [256], P('seq'), may hold values from 0 to 999
- offsets: int32 [256], P('seq'), may hold values from -64 to 64, as said below
- teacher_heads: bfloat16 [16384, 2560], P('seq', 'tp'), may hold values from -6 to 6
- teacher_proj: bfloat16 [2560, 5120], P('tp', 'seq'), may hold values from -0.125 to 0.125
- queries: bfloat16 [16384, 2560], P('seq', 'tp'), may hold values from -200 to 200
- keys: bfloat16 [16384, 2560], P('seq', 'tp'), may hold values from -6 to 6
- values: bfloat16 [16384, 2560], P('seq', 'tp'), may hold values from -6 to 6
- query_tangent: bfloat16 [16384, 2560], P('seq', 'tp'), may hold values from -6 to 6
- key_tangent: bfloat16 [16384, 2560], P('seq', 'tp'), may hold values from -6 to 6
- value_tangent: bfloat16 [16384, 2560], P('seq', 'tp'), may hold values from -6 to 6
- out_proj: bfloat16 [2560, 5120], P('tp', 'seq'), may hold values from -0.125 to 0.125
Outputs:
- student_out: float32 [16384, 5120], P('seq', 'tp')
- student_tangent: float32 [16384, 5120], P('seq', 'tp')
Inputs may be any that keep to these rules, and one draw needn't show every extreme that they name: `offsets`: both ends, -64 and 64, occur in every draw.
All inputs are finite; a program needn't handle non-finite values.
Results may differ from a plain program's by a relative error of at most 0.0045.
Values may be sent and summed in bfloat16 or wider, within the bound.
No kernel may reach another device: no remote copies, remote signals or barrier semaphores. Data moves between devices by JAX's collectives and lax.ppermute only.
A program may use at most 128 MiB of HBM per device.

v0:
```python
import functools
import math

import jax
import jax.numpy as jnp
from jax import lax
from jax.experimental import pallas as pl
from jax.experimental.pallas import tpu as pltpu
from jax.sharding import PartitionSpec as P


HD = 128
WIN = 256
OFF = 64
BLK = 64
STEPS = 1000
REACH = WIN // 2 + OFF
AXES = ("seq", "tp")
NZ, NY, NX, NT = 8, 4, 2, 4


def flat(z, y, x, t):
    return (((z % NZ) * NY + y % NY) * NX + x % NX) * NT + t


def pairs(move):
    return [
        (flat(z, y, x, t), flat(*move(z, y, x, t)))
        for z in range(NZ)
        for y in range(NY)
        for x in range(NX)
        for t in range(NT)
    ]


def send(a, move):
    return lax.ppermute(a, AXES, pairs(move))


def z_by(d):
    return lambda z, y, x, t: (z + d, y, x, t)


def y_by(d):
    return lambda z, y, x, t: (z, y + d, x, t)


def t_xor(k):
    return lambda z, y, x, t: (z, y, x, t ^ k)


def swap_zt(flip):
    def move(z, y, x, t):
        m = t ^ (z >> 1)
        return ((z >> 1) * 2 + (m + 1 if z & 1 else -m), y, x ^ flip, z >> 1)

    return move


NT_DIMS = (((1,), (1,)), ((), ()))
NN_DIMS = (((1,), (0,)), ((), ()))
HALF = 640
PAIR = 160
YD = (0, -1, 1, 2)


def attn_kernel(where, offs, q, qd, k, v, kd, vd, low, high, out, pad, sems):
    tokens, width = q.shape
    span = tokens + 2 * REACH
    copies = []
    for n, i in enumerate((0, 2, 1, 3)):
        own = (k, v, kd, vd)[i]
        parts = (
            (own, pad.at[i, pl.ds(REACH, tokens)]),
            (low.at[i], pad.at[i, pl.ds(0, REACH)]),
            (high.at[i], pad.at[i, pl.ds(REACH + tokens, REACH)]),
        )
        for j, (src, dst) in enumerate(parts):
            copies.append(pltpu.make_async_copy(src, dst, sems.at[3 * n + j]))
    for c in copies:
        c.start()
    scale = 1.0 / math.sqrt(HD)
    first = where[0] * tokens
    total = where[1] * tokens
    ki = lax.broadcasted_iota(jnp.int32, (tokens, span), 1) - REACH
    qi = lax.broadcasted_iota(jnp.int32, (tokens, 1), 0)
    off = jnp.zeros((tokens, 1), jnp.int32) + offs[0]
    for b in range(1, tokens // BLK):
        off = jnp.where(qi >= b * BLK, offs[b], off)
    begin = qi + off - WIN // 2
    lower = jnp.maximum(begin, -first)
    upper = jnp.minimum(begin + WIN, total - first)
    inside = (ki >= lower) & (ki < upper)
    for c in copies[:6]:
        c.wait()
    for c in copies[6:]:
        c.wait()

    def head(h, carry):
        cols = pl.ds(pl.multiple_of(h * HD, HD), HD)
        qb = q[:, cols]
        both = jnp.concatenate([qb, qd[:, cols]], axis=0)
        s2 = lax.dot_general(both, pad[0, :, cols], NT_DIMS, preferred_element_type=jnp.float32)
        s3 = lax.dot_general(qb, pad[2, :, cols], NT_DIMS, preferred_element_type=jnp.float32)
        s = jnp.where(inside, s2[:tokens] * scale, -1e30)
        e = jnp.exp(s - jnp.max(s, axis=-1, keepdims=True))
        w = e * (1.0 / jnp.sum(e, axis=-1, keepdims=True))
        sd = (s2[tokens:] + s3) * scale
        wd = w * (sd - jnp.sum(w * sd, axis=-1, keepdims=True))
        wl = w.astype(jnp.bfloat16)
        wb = jnp.concatenate([wl, wd.astype(jnp.bfloat16)], axis=0)
        o2 = lax.dot_general(wb, pad[1, :, cols], NN_DIMS, preferred_element_type=jnp.float32)
        o3 = lax.dot_general(wl, pad[3, :, cols], NN_DIMS, preferred_element_type=jnp.float32)
        out[:tokens, cols] = o2[:tokens].astype(jnp.bfloat16)
        out[tokens:, cols] = (o2[tokens:] + o3).astype(jnp.bfloat16)
        return carry

    lax.fori_loop(0, width // HD, head, 0)


def rows_of(where, dy):
    return pl.ds(pl.multiple_of(((where[1] + dy) & 3) * PAIR, 32), PAIR)


def sources(z, t):
    gap = (z + jnp.array((0, -1, 1, -2, 2, -3, 3, 4), jnp.int32) - 2 * t) & 7
    upper = (gap >= 1) & (gap <= 4)
    return [jnp.where(upper, gap - 1, (8 - gap) & 7), upper.astype(jnp.int32)]


def accumulate(where, x, w, i, acc):
    kb = where[4 + i]
    hf = where[12 + i]
    acc[hf] += lax.dot_general(x[kb], w[i], NT_DIMS, preferred_element_type=jnp.float32)


def tea_kernel(spans, *refs):
    where, vel = refs[0], refs[5 + 4 * len(spans)]
    ths = refs[1:5]
    wy, tea, sem_y, sem_t = refs[-4:]
    heads = [pltpu.make_async_copy(ths[j], tea.at[j], sem_t.at[j]) for j in range(4)]
    for c in heads:
        c.start()
    base = spans[0][0]
    for i, (lo, n) in enumerate(spans):
        for j, dy in enumerate(YD):
            dst = wy.at[pl.ds(lo - base, n), rows_of(where, dy)]
            pltpu.make_async_copy(refs[5 + 4 * i + j], dst, sem_y.at[i]).start()
    if base:
        before, vel = vel, refs[6 + 4 * len(spans)]
        vel[...] = before[...]
    else:
        vel[...] = jnp.zeros_like(vel)
    for c in heads:
        c.wait()
    for i, (lo, n) in enumerate(spans):
        part = wy.at[pl.ds(lo - base, n)]
        pltpu.make_async_copy(part, part, sem_y.at[i]).wait()

        def step(k, carry):
            kb = where[4 + k]
            hf = where[12 + k]
            vel[hf] += lax.dot_general(
                tea[kb], wy[k - base], NT_DIMS, preferred_element_type=jnp.float32
            )
            return carry

        lax.fori_loop(lo, lo + n, step, 0)


def mid_kernel(*refs):
    where = refs[0]
    ats = refs[1:5]
    za = refs[5:12]
    zb = refs[12:19]
    acc = refs[19]
    wz, att, sem_z, sem_a = refs[20:]
    heads = [pltpu.make_async_copy(ats[j], att.at[j], sem_a.at[j]) for j in range(4)]
    for c in heads:
        c.start()
    for i in range(7):
        for j, dy in enumerate(YD):
            buf = (za, zb)[j // 2][i]
            dst = wz.at[i, rows_of(where, dy)]
            pltpu.make_async_copy(buf.at[j % 2], dst, sem_z.at[i]).start()
    acc[...] = jnp.zeros_like(acc)
    for c in heads:
        c.wait()

    def step(k, carry):
        pltpu.make_async_copy(wz.at[k], wz.at[k], sem_z.at[k]).wait()
        accumulate(where, att, wz, k, acc)
        return carry

    lax.fori_loop(0, 7, step, 0)


def last_kernel(*refs):
    where, trig = refs[:2]
    ats = refs[2:6]
    z4 = refs[6:8]
    more = refs[8:10]
    acc, vel = refs[10:12]
    outs = refs[12:14]
    wz, att, lat, noi, p, res, sem_z, sem_a, sem_m, sem_o = refs[14:]
    kb = where[11]
    for j, dy in enumerate(YD):
        pltpu.make_async_copy(z4[j // 2].at[j % 2], wz.at[rows_of(where, dy)], sem_z.at[0]).start()
    for j in range(4):

        @pl.when(kb == j)
        def _():
            pltpu.make_async_copy(ats[j], att, sem_a.at[0]).start()

    extra = [
        pltpu.make_async_copy(s, d, sem_m.at[i]) for i, (s, d) in enumerate(zip(more, (lat, noi)))
    ]
    for c in extra:
        c.start()
    pltpu.make_async_copy(ats[0], att, sem_a.at[0]).wait()
    pltpu.make_async_copy(wz, wz, sem_z.at[0]).wait()
    p[...] = lax.dot_general(att[...], wz[...], NT_DIMS, preferred_element_type=jnp.float32)
    for c in extra:
        c.wait()
    tokens = lat.shape[0]
    stores = []
    for hf in range(2):
        cols = slice(hf * HALF, (hf + 1) * HALF)
        on = (where[19] == hf).astype(jnp.float32)

        def block(b, carry):
            start = pl.multiple_of(b * BLK, BLK)
            rows = pl.ds(start, BLK)
            low = pl.ds(pl.multiple_of(tokens + start, BLK), BLK)
            c = trig[0, b]
            s = trig[1, b]
            noisy = c * lat[rows, cols].astype(jnp.float32) + s * noi[rows, cols].astype(jnp.float32)
            br = acc[hf, rows] + on * p[rows]
            bt = acc[hf, low] + on * p[low]
            res[0, hf, rows] = c * noisy - s * br
            res[1, hf, rows] = c * vel[hf, rows] - s * noisy - c * br - s * bt
            return carry

        lax.fori_loop(0, tokens // BLK, block, 0)
        for k in range(2):
            dst = outs[k].at[:, pl.ds(hf * HALF, HALF)]
            stores.append(pltpu.make_async_copy(res.at[k, hf], dst, sem_o.at[2 * hf + k]))
            stores[-1].start()
    for c in stores:
        c.wait()


def body(
    latents,
    noise,
    tstep,
    offsets,
    teacher_heads,
    teacher_proj,
    queries,
    keys,
    values,
    query_tangent,
    key_tangent,
    value_tangent,
    out_proj,
):
    tokens, width = queries.shape
    seq = lax.axis_index("seq").astype(jnp.int32)
    tp = lax.axis_index("tp").astype(jnp.int32)
    count = lax.axis_size("seq")
    step_time = (tstep.astype(jnp.float32) + 0.5) * (math.pi / (2 * STEPS))
    trig = jnp.stack([jnp.cos(step_time), jnp.sin(step_time)])
    bf = jnp.bfloat16

    arrays = (keys, values, key_tangent, value_tangent)
    fwd = [(i, i + 1) for i in range(count - 1)]
    bwd = [(i + 1, i) for i in range(count - 1)]
    low = lax.ppermute(jnp.stack([a[tokens - REACH :] for a in arrays]), "seq", fwd)
    high = lax.ppermute(jnp.stack([a[:REACH] for a in arrays]), "seq", bwd)

    small = jnp.stack([out_proj.T, teacher_proj.T])
    p0 = send(small, swap_zt(0))
    p1 = send(small, swap_zt(1))
    even = seq % 2 == 0
    unit = jnp.concatenate([jnp.where(even, p0, p1), jnp.where(even, p1, p0)], axis=1)
    oz = unit[0]
    ty = unit[1]

    th = [teacher_heads]
    th.append(send(teacher_heads, t_xor(1)))
    th.append(send(teacher_heads, t_xor(2)))
    th.append(send(th[2], t_xor(1)))

    yp = send(oz, y_by(1))
    ym = send(oz, y_by(-1))
    y2 = send(yp, y_by(1))

    def over_z(buf, up):
        p = [buf]
        m = [buf]
        for _ in range(3):
            p.append(send(p[-1], z_by(1)))
            m.append(send(m[-1], z_by(-1)))
        end = send(p[3] if up else m[3], z_by(1 if up else -1))
        return [buf, p[1], m[1], p[2], m[2], p[3], m[3]], end

    za, za4 = over_z(jnp.stack([oz, yp]), True)
    zb, zb4 = over_z(jnp.stack([ym, y2]), False)

    zp = [ty]
    zm = [ty]
    for _ in range(3):
        zp.append(send(zp[-1], z_by(1)))
        zm.append(send(zm[-1], z_by(-1)))
    z4 = send(zp[3], z_by(1))

    def over_y(parts, up):
        buf = jnp.stack(parts)
        p = send(buf, y_by(1))
        m = send(buf, y_by(-1))
        end = send(p if up else m, y_by(1 if up else -1))
        return [buf, p, m, end]

    sets = over_y([ty, zp[1], zm[1]], False)
    sets += over_y([zp[2], zm[2]], True)
    sets += over_y([zp[3], zm[3], z4], True)

    vm = pl.BlockSpec(memory_space=pltpu.VMEM)
    sm = pl.BlockSpec(memory_space=pltpu.SMEM)
    hb = pl.BlockSpec(memory_space=pl.ANY)
    dma = pltpu.SemaphoreType.DMA
    f32 = jnp.float32
    attended = pl.pallas_call(
        attn_kernel,
        out_shape=jax.ShapeDtypeStruct((2 * tokens, width), bf),
        in_specs=[sm, sm, vm, vm] + [hb] * 6,
        out_specs=vm,
        scratch_shapes=[pltpu.VMEM((4, tokens + 2 * REACH, width), bf), dma((12,))],
        compiler_params=pltpu.CompilerParams(vmem_limit_bytes=20 << 20),
        name="attend",
    )(
        jnp.stack([seq, jnp.int32(count)]),
        offsets,
        queries,
        query_tangent,
        *arrays,
        low,
        high,
    )
    at = [attended]
    at.append(send(attended, t_xor(1)))
    at.append(send(attended, t_xor(2)))
    at.append(send(at[2], t_xor(1)))

    cols = latents.shape[1]
    where = jnp.concatenate(
        [jnp.stack([seq // 8, (seq // 2) % 4, seq % 2, tp])] + sources(seq // 8, tp)
    )
    full = jax.ShapeDtypeStruct((2, 2 * tokens, HALF), f32)
    half = jax.ShapeDtypeStruct((2, tokens, HALF), f32)

    def run(kernel, out_shape, ins, specs, outs, scratch):
        return pl.pallas_call(
            kernel,
            out_shape=out_shape,
            in_specs=specs,
            out_specs=outs,
            scratch_shapes=scratch,
            compiler_params=pltpu.CompilerParams(vmem_limit_bytes=16 << 20),
        )(*ins)

    def teach(spans, bufs, *before):
        total = sum(n for _, n in spans)
        return run(
            functools.partial(tea_kernel, spans),
            half,
            (where, *th, *bufs, *before),
            [sm] + [hb] * (4 + len(bufs)) + [vm] * len(before),
            vm,
            [
                pltpu.VMEM((total, HALF, width), bf),
                pltpu.VMEM((4, tokens, width), bf),
                dma((len(spans),)),
                dma((4,)),
            ],
        )

    vel = teach(SPANS[:CUT], sets[: 4 * CUT])
    vel = teach(SPANS[CUT:], sets[4 * CUT :], vel)
    acc = run(
        mid_kernel,
        full,
        (where, *at, *za, *zb),
        [sm] + [hb] * 18,
        vm,
        [
            pltpu.VMEM((7, HALF, width), bf),
            pltpu.VMEM((4, 2 * tokens, width), bf),
            dma((7,)),
            dma((4,)),
        ],
    )
    return run(
        last_kernel,
        (jax.ShapeDtypeStruct((tokens, cols), f32),) * 2,
        (where, trig, *at, za4, zb4, latents, noise, acc, vel),
        [sm, sm] + [hb] * 8 + [vm] * 2,
        (hb, hb),
        [
            pltpu.VMEM((HALF, width), bf),
            pltpu.VMEM((2 * tokens, width), bf),
            pltpu.VMEM((tokens, cols), bf),
            pltpu.VMEM((tokens, cols), bf),
            pltpu.VMEM((2 * tokens, HALF), f32),
            pltpu.VMEM((2, 2, tokens, HALF), f32),
            dma((1,)),
            dma((1,)),
            dma((2,)),
            dma((4,)),
        ],
    )


SPANS = ((0, 3), (3, 2), (5, 3))
CUT = 2


def solution(mesh):
    return jax.shard_map(
        body,
        mesh=mesh,
        in_specs=(
            P("seq", "tp"),
            P("seq", "tp"),
            P("seq"),
            P("seq"),
            P("seq", "tp"),
            P("tp", "seq"),
            P("seq", "tp"),
            P("seq", "tp"),
            P("seq", "tp"),
            P("seq", "tp"),
            P("seq", "tp"),
            P("seq", "tp"),
            P("tp", "seq"),
        ),
        out_specs=(P("seq", "tp"), P("seq", "tp")),
        check_vma=False,
    )
```

profile of v0, /device:TPU:28, one launch (start us, length us, event | category | flops | bytes accessed | tf_op | source)
XLA Modules:
  0.0 201.6 jit_solution(17954839975844621729)
XLA Ops:
  2.9 9.5 %collective-permute-start.25 = (bf16[256,640]{1,0:T(8,128)(2,1)}, bf16[256,640]{1,0:T(8,128)(2,1)S(1)}, u32[]{:S(2)}, u32[]{:S(2)}) collective-permute-start(bf16[256,640]{1,0:T(8,128)(2,1)} %refs_1_.3), channel_id=1, source_target_pairs={{0,2},{1,3},{2,0},{3,1},{4,6},{5,7},{6,4},{7,5},{8,10},{9,11},{10,... | collective-permute-start | bytes 983048 | tf_op jit(solution)/shard_map/ppermute | solution.py:37
  15.3 8.1 %collective-permute-start.30 = (bf16[160,640]{1,0:T(8,128)(2,1)S(1)}, bf16[160,640]{1,0:T(8,128)(2,1)S(1)}, u32[]{:S(2)}, u32[]{:S(2)}) collective-permute-start(bf16[160,640]{1,0:T(8,128)(2,1)S(1)} %bitcast.44), channel_id=1, source_target_pairs={{0,224},{1,225},{2,226},{3,227},{4,228},{5,229},{6,230},{7,231},{8... | collective-permute-start | bytes 614408 | tf_op jit(solution)/shard_map/ppermute | solution.py:37
  30.9 9.0 %collective-permute-start.31 = (bf16[160,640]{1,0:T(8,128)(2,1)S(1)}, bf16[160,640]{1,0:T(8,128)(2,1)S(1)}, u32[]{:S(2)}, u32[]{:S(2)}) collective-permute-start(bf16[160,640]{1,0:T(8,128)(2,1)S(1)} %collective-permute-done.30), channel_id=1, source_target_pairs={{0,224},{1,225},{2,226},{3,227},{4,228},{5,229},{6,230},{7,231},{8... | collective-permute-start | bytes 614408 | tf_op jit(solution)/shard_map/ppermute | solution.py:37
  47.0 3.2 %collective-permute-start.32 = (bf16[160,640]{1,0:T(8,128)(2,1)S(1)}, bf16[160,640]{1,0:T(8,128)(2,1)S(1)}, u32[]{:S(2)}, u32[]{:S(2)}) collective-permute-start(bf16[160,640]{1,0:T(8,128)(2,1)S(1)} %collective-permute-done.31), channel_id=1, source_target_pairs={{0,224},{1,225},{2,226},{3,227},{4,228},{5,229},{6,230},{7,231},{8... | collective-permute-start | bytes 614408 | tf_op jit(solution)/shard_map/ppermute | solution.py:37
  50.3 26.5 %collective-permute-done.29 = bf16[160,640]{1,0:T(8,128)(2,1)S(1)} collective-permute-done((bf16[160,640]{1,0:T(8,128)(2,1)S(1)}, bf16[160,640]{1,0:T(8,128)(2,1)S(1)}, u32[]{:S(2)}, u32[]{:S(2)}) %collective-permute-start.29) | collective-permute-done | bytes 204832 | tf_op jit(solution)/shard_map/ppermute | solution.py:37
  76.8 7.2 %collective-permute-start.18 = (bf16[2,160,640]{2,1,0:T(8,128)(2,1)S(1)}, bf16[2,160,640]{2,1,0:T(8,128)(2,1)S(1)}, u32[]{:S(2)}, u32[]{:S(2)}) collective-permute-start(bf16[2,160,640]{2,1,0:T(8,128)(2,1)S(1)} %pad_maximum_fusion.4.refs_5_), channel_id=1, source_target_pairs={{0,224},{1,225},{2,226},{3,227},{4,228},{5,229},{6,230},{7,231},{8... | collective-permute-start | bytes 1228808 | tf_op jit(solution)/shard_map/ppermute | solution.py:37
  84.2 3.2 %collective-permute-start.37 = (bf16[3,160,640]{2,1,0:T(8,128)(2,1)S(1)}, bf16[3,160,640]{2,1,0:T(8,128)(2,1)S(1)}, u32[]{:S(2)}, u32[]{:S(2)}) collective-permute-start(bf16[3,160,640]{2,1,0:T(8,128)(2,1)S(1)} %pad_maximum_fusion.3.refs_5_), channel_id=1, source_target_pairs={{0,8},{1,9},{2,10},{3,11},{4,12},{5,13},{6,14},{7,15},{8,16},{9,17... | collective-permute-start | bytes 1843208 | tf_op jit(solution)/shard_map/ppermute | solution.py:37
  87.5 4.6 %collective-permute-done.18.refs_7_ = bf16[2,160,640]{2,1,0:T(8,128)(2,1)S(1)} collective-permute-done((bf16[2,160,640]{2,1,0:T(8,128)(2,1)S(1)}, bf16[2,160,640]{2,1,0:T(8,128)(2,1)S(1)}, u32[]{:S(2)}, u32[]{:S(2)}) %collective-permute-start.18) | collective-permute-done | bytes 409632 | tf_op jit(solution)/shard_map/ppermute | solution.py:37
  94.3 3.8 %collective-permute-start.14 = (bf16[2,160,640]{2,1,0:T(8,128)(2,1)S(1)}, bf16[2,160,640]{2,1,0:T(8,128)(2,1)S(1)}, u32[]{:S(2)}, u32[]{:S(2)}) collective-permute-start(bf16[2,160,640]{2,1,0:T(8,128)(2,1)S(1)} %pad_maximum_fusion.5.refs_12_), channel_id=1, source_target_pairs={{0,224},{1,225},{2,226},{3,227},{4,228},{5,229},{6,230},{7,231},{8... | collective-permute-start | bytes 1228808 | tf_op jit(solution)/shard_map/ppermute | solution.py:37
  98.1 4.1 %collective-permute-done.38.refs_7_ = bf16[3,160,640]{2,1,0:T(8,128)(2,1)S(1)} collective-permute-done((bf16[3,160,640]{2,1,0:T(8,128)(2,1)S(1)}, bf16[3,160,640]{2,1,0:T(8,128)(2,1)S(1)}, u32[]{:S(2)}, u32[]{:S(2)}) %collective-permute-start.38) | collective-permute-done | bytes 614432 | tf_op jit(solution)/shard_map/ppermute | solution.py:37
  103.0 5.2 %collective-permute-done.40.refs_10_ = bf16[2,160,640]{2,1,0:T(8,128)(2,1)S(1)} collective-permute-done((bf16[2,160,640]{2,1,0:T(8,128)(2,1)S(1)}, bf16[2,160,640]{2,1,0:T(8,128)(2,1)S(1)}, u32[]{:S(2)}, u32[]{:S(2)}) %collective-permute-start.40) | collective-permute-done | bytes 409632 | tf_op jit(solution)/shard_map/ppermute | solution.py:37
  112.9 3.7 %collective-permute-start.42 = (bf16[2,160,640]{2,1,0:T(8,128)(2,1)S(1)}, bf16[2,160,640]{2,1,0:T(8,128)(2,1)S(1)}, u32[]{:S(2)}, u32[]{:S(2)}) collective-permute-start(bf16[2,160,640]{2,1,0:T(8,128)(2,1)S(1)} %collective-permute-done.40.refs_10_), channel_id=1, source_target_pairs={{0,8},{1,9},{2,10},{3,11},{4,12},{5,13},{6,14},{7,15},{8,16},{9,17... | collective-permute-start | bytes 1228808 | tf_op jit(solution)/shard_map/ppermute | solution.py:37
  119.7 5.4 %collective-permute-done.9.refs_8_ = bf16[2,160,640]{2,1,0:T(8,128)(2,1)} collective-permute-done((bf16[2,160,640]{2,1,0:T(8,128)(2,1)S(1)}, bf16[2,160,640]{2,1,0:T(8,128)(2,1)}, u32[]{:S(2)}, u32[]{:S(2)}) %collective-permute-start.9) | collective-permute-done | bytes 409632 | tf_op jit(solution)/shard_map/ppermute | solution.py:37
  127.4 8.9 %attend.1.refs_1_.refs_2_ = bf16[512,640]{1,0:T(8,128)(2,1)S(1)} custom-call(s32[2]{0:T(128)S(1)} %pad_add_fusion.where, s32[4]{0:T(128)S(1)} %copy-done.47, bf16[256,640]{1,0:T(8,128)(2,1)S(1)} %copy-done.45, bf16[256,640]{1,0:T(8,128)(2,1)S(1)} %copy-done.46, bf16[256,640]{1,0:T(8,128)(2,1)S(1)} %copy-done.2, bf16[256,640]{1,0:T(8,128)(2,1)S(1)} %copy-done.3, ...), custom_call_target="tpu_custom_call" | custom-call | tf_op jit(solution)/shard_map/attend/pallas_call | solution.py:334
  136.6 3.8 %collective-permute-start.36 = (bf16[3,160,640]{2,1,0:T(8,128)(2,1)}, bf16[3,160,640]{2,1,0:T(8,128)(2,1)}, u32[]{:S(2)}, u32[]{:S(2)}) collective-permute-start(bf16[3,160,640]{2,1,0:T(8,128)(2,1)} %collective-permute-done.34.refs_6_), channel_id=1, source_target_pairs={{0,8},{1,9},{2,10},{3,11},{4,12},{5,13},{6,14},{7,15},{8,16},{9,17... | collective-permute-start | bytes 1843208 | tf_op jit(solution)/shard_map/ppermute | solution.py:37
  143.8 3.1 %collective-permute-start.20 = (bf16[2,160,640]{2,1,0:T(8,128)(2,1)}, bf16[2,160,640]{2,1,0:T(8,128)(2,1)}, u32[]{:S(2)}, u32[]{:S(2)}) collective-permute-start(bf16[2,160,640]{2,1,0:T(8,128)(2,1)} %collective-permute-done.19.refs_9_), channel_id=1, source_target_pairs={{0,224},{1,225},{2,226},{3,227},{4,228},{5,229},{6,230},{7,231},{8... | collective-permute-start | bytes 1228808 | tf_op jit(solution)/shard_map/ppermute | solution.py:37
  146.9 2.8 %collective-permute-done.35.refs_7_ = bf16[3,160,640]{2,1,0:T(8,128)(2,1)S(1)} collective-permute-done((bf16[3,160,640]{2,1,0:T(8,128)(2,1)S(1)}, bf16[3,160,640]{2,1,0:T(8,128)(2,1)S(1)}, u32[]{:S(2)}, u32[]{:S(2)}) %collective-permute-start.35) | collective-permute-done | bytes 614432 | tf_op jit(solution)/shard_map/ppermute | solution.py:37
  150.6 3.0 %collective-permute-start.16 = (bf16[2,160,640]{2,1,0:T(8,128)(2,1)}, bf16[2,160,640]{2,1,0:T(8,128)(2,1)}, u32[]{:S(2)}, u32[]{:S(2)}) collective-permute-start(bf16[2,160,640]{2,1,0:T(8,128)(2,1)} %collective-permute-done.15.refs_16_), channel_id=1, source_target_pairs={{0,224},{1,225},{2,226},{3,227},{4,228},{5,229},{6,230},{7,231},{8... | collective-permute-start | bytes 1228808 | tf_op jit(solution)/shard_map/ppermute | solution.py:37
  156.2 5.5 %collective-permute-done.16.refs_18_ = bf16[2,160,640]{2,1,0:T(8,128)(2,1)} collective-permute-done((bf16[2,160,640]{2,1,0:T(8,128)(2,1)}, bf16[2,160,640]{2,1,0:T(8,128)(2,1)}, u32[]{:S(2)}, u32[]{:S(2)}) %collective-permute-start.16) | collective-permute-done | bytes 409632 | tf_op jit(solution)/shard_map/ppermute | solution.py:37
  161.7 3.7 %collective-permute-start.17 = (bf16[2,160,640]{2,1,0:T(8,128)(2,1)}, bf16[2,160,640]{2,1,0:T(8,128)(2,1)}, u32[]{:S(2)}, u32[]{:S(2)}) collective-permute-start(bf16[2,160,640]{2,1,0:T(8,128)(2,1)} %collective-permute-done.16.refs_18_), channel_id=1, source_target_pairs={{0,224},{1,225},{2,226},{3,227},{4,228},{5,229},{6,230},{7,231},{8... | collective-permute-start | bytes 1228808 | tf_op jit(solution)/shard_map/ppermute | solution.py:37
  177.7 4.1 %shard_map.150.refs_9_ = f32[2,256,640]{2,1,0:T(8,128)S(1)} custom-call(s32[20]{0:T(128)S(1)} %concatenate.6.refs_0_, bf16[256,640]{1,0:T(8,128)(2,1)S(1)} %copy-done.12, bf16[256,640]{1,0:T(8,128)(2,1)S(1)} %copy-done.16, bf16[256,640]{1,0:T(8,128)(2,1)S(1)} %copy-done.14, bf16[256,640]{1,0:T(8,128)(2,1)S(1)} %copy-done.18, ...), custom_call_target="tpu_custom_call" | custom-call | tf_op jit(solution)/shard_map/pallas_call | solution.py:364
  181.9 3.7 %shard_map.151.refs_11_ = f32[2,256,640]{2,1,0:T(8,128)S(1)} custom-call(s32[20]{0:T(128)S(1)} %concatenate.6.refs_0_, bf16[256,640]{1,0:T(8,128)(2,1)S(1)} %copy-done.12, bf16[256,640]{1,0:T(8,128)(2,1)S(1)} %copy-done.16, bf16[256,640]{1,0:T(8,128)(2,1)S(1)} %copy-done.14, bf16[256,640]{1,0:T(8,128)(2,1)S(1)} %copy-done.18, ...), custom_call_target="tpu_custom_call" | custom-call | tf_op jit(solution)/shard_map/pallas_call | solution.py:364
  185.8 11.0 %shard_map.149.refs_10_ = f32[2,512,640]{2,1,0:T(8,128)S(1)} custom-call(s32[20]{0:T(128)S(1)} %concatenate.6.refs_0_, bf16[512,640]{1,0:T(8,128)(2,1)S(1)} %attend.1.refs_1_.refs_2_, bf16[512,640]{1,0:T(8,128)(2,1)S(1)} %collective-permute-done.2.refs_2_.refs_3_, bf16[512,640]{1,0:T(8,128)(2,1)S(1)} %collective-permute-done.3.refs_3_.refs_4_, ...), custom_call_target="tpu_custom_call" | custom-call | tf_op jit(solution)/shard_map/pallas_call | solution.py:364
  196.8 4.6 %shard_map.152 = (f32[256,1280]{1,0:T(8,128)}, f32[256,1280]{1,0:T(8,128)}) custom-call(s32[20]{0:T(128)S(1)} %concatenate.6.refs_0_, f32[2,4]{1,0:T(2,128)S(1)} %pad_maximum_fusion.9.refs_1_, bf16[512,640]{1,0:T(8,128)(2,1)S(1)} %attend.1.refs_1_.refs_2_, bf16[512,640]{1,0:T(8,128)(2,1)S(1)} %collective-permute-done.2.refs_2_.refs_3_, ...), custom_call_target="tpu_custom_call" | custom-call | tf_op jit(solution)/shard_map/pallas_call | solution.py:364
  (185 shorter events, 52.3 us)
Async XLA Ops:
  2.9 20.8 %collective-permute-start.25 = (bf16[256,640]{1,0:T(8,128)(2,1)}, bf16[256,640]{1,0:T(8,128)(2,1)S(1)}, u32[]{:S(2)}, u32[]{:S(2)}) collective-permute-start(bf16[256,640]{1,0:T(8,128)(2,1)} %refs_1_.3), channel_id=1, source_target_pairs={{0,2},{1,3},{2,0},{3,1},{4,6},{5,7},{6,4},{7,5},{8,10},{9,11},{10,... | collective-permute-start | bytes 983048 | tf_op jit(solution)/shard_map/ppermute | solution.py:37
  27.8 64.4 %collective-permute-start.1 = (bf16[4,192,640]{2,1,0:T(8,128)(2,1)S(1)}, bf16[4,192,640]{2,1,0:T(8,128)(2,1)S(1)}, u32[]{:S(2)}, u32[]{:S(2)}) collective-permute-start(bf16[4,192,640]{2,1,0:T(8,128)(2,1)S(1)} %pad_maximum_fusion.1), channel_id=1, source_target_pairs={{4,0},{8,4},{12,8},{16,12},{20,16},{24,20},{28,24},{32,28},{36,32}... | collective-permute-start | bytes 2949128 | tf_op jit(solution)/shard_map/ppermute | solution.py:280
  29.8 17.2 %collective-permute-start.26 = (bf16[256,640]{1,0:T(8,128)(2,1)S(1)}, bf16[256,640]{1,0:T(8,128)(2,1)S(1)}, u32[]{:S(2)}, u32[]{:S(2)}) collective-permute-start(bf16[256,640]{1,0:T(8,128)(2,1)S(1)} %collective-permute-done.25.refs_3_), channel_id=1, source_target_pairs={{0,1},{1,0},{2,3},{3,2},{4,5},{5,4},{6,7},{7,6},{8,9},{9,8},{10,11... | collective-permute-start | bytes 983048 | tf_op jit(solution)/shard_map/ppermute | solution.py:37
  40.2 54.1 %collective-permute-start = (bf16[4,192,640]{2,1,0:T(8,128)(2,1)S(1)}, bf16[4,192,640]{2,1,0:T(8,128)(2,1)S(1)}, u32[]{:S(2)}, u32[]{:S(2)}) collective-permute-start(bf16[4,192,640]{2,1,0:T(8,128)(2,1)S(1)} %pad_maximum_fusion), channel_id=1, source_target_pairs={{0,4},{4,8},{8,12},{12,16},{16,20},{20,24},{24,28},{28,32},{32,36}... | collective-permute-start | bytes 2949128 | tf_op jit(solution)/shard_map/ppermute | solution.py:279
  44.8 39.4 %collective-permute-start.8 = (bf16[2,160,640]{2,1,0:T(8,128)(2,1)S(1)}, bf16[2,160,640]{2,1,0:T(8,128)(2,1)S(1)}, u32[]{:S(2)}, u32[]{:S(2)}) collective-permute-start(bf16[2,160,640]{2,1,0:T(8,128)(2,1)S(1)} %pad_maximum_fusion.4.refs_5_), channel_id=1, source_target_pairs={{0,32},{1,33},{2,34},{3,35},{4,36},{5,37},{6,38},{7,39},{8,40},{9,... | collective-permute-start | bytes 1228808 | tf_op jit(solution)/shard_map/ppermute | solution.py:37
  47.0 29.8 %collective-permute-start.29 = (bf16[160,640]{1,0:T(8,128)(2,1)S(1)}, bf16[160,640]{1,0:T(8,128)(2,1)S(1)}, u32[]{:S(2)}, u32[]{:S(2)}) collective-permute-start(bf16[160,640]{1,0:T(8,128)(2,1)S(1)} %collective-permute-done.28), channel_id=1, source_target_pairs={{0,32},{1,33},{2,34},{3,35},{4,36},{5,37},{6,38},{7,39},{8,40},{9,... | collective-permute-start | bytes 614408 | tf_op jit(solution)/shard_map/ppermute | solution.py:37
  47.0 37.1 %collective-permute-start.32 = (bf16[160,640]{1,0:T(8,128)(2,1)S(1)}, bf16[160,640]{1,0:T(8,128)(2,1)S(1)}, u32[]{:S(2)}, u32[]{:S(2)}) collective-permute-start(bf16[160,640]{1,0:T(8,128)(2,1)S(1)} %collective-permute-done.31), channel_id=1, source_target_pairs={{0,224},{1,225},{2,226},{3,227},{4,228},{5,229},{6,230},{7,231},{8... | collective-permute-start | bytes 614408 | tf_op jit(solution)/shard_map/ppermute | solution.py:37
  84.1 18.0 %collective-permute-start.38 = (bf16[3,160,640]{2,1,0:T(8,128)(2,1)S(1)}, bf16[3,160,640]{2,1,0:T(8,128)(2,1)S(1)}, u32[]{:S(2)}, u32[]{:S(2)}) collective-permute-start(bf16[3,160,640]{2,1,0:T(8,128)(2,1)S(1)} %pad_maximum_fusion.3.refs_5_), channel_id=1, source_target_pairs={{0,24},{1,25},{2,26},{3,27},{4,28},{5,29},{6,30},{7,31},{8,0},{9,1... | collective-permute-start | bytes 1843208 | tf_op jit(solution)/shard_map/ppermute | solution.py:37
  84.2 17.9 %collective-permute-start.37 = (bf16[3,160,640]{2,1,0:T(8,128)(2,1)S(1)}, bf16[3,160,640]{2,1,0:T(8,128)(2,1)S(1)}, u32[]{:S(2)}, u32[]{:S(2)}) collective-permute-start(bf16[3,160,640]{2,1,0:T(8,128)(2,1)S(1)} %pad_maximum_fusion.3.refs_5_), channel_id=1, source_target_pairs={{0,8},{1,9},{2,10},{3,11},{4,12},{5,13},{6,14},{7,15},{8,16},{9,17... | collective-permute-start | bytes 1843208 | tf_op jit(solution)/shard_map/ppermute | solution.py:37
  92.2 16.8 %collective-permute-start.41 = (bf16[2,160,640]{2,1,0:T(8,128)(2,1)S(1)}, bf16[2,160,640]{2,1,0:T(8,128)(2,1)S(1)}, u32[]{:S(2)}, u32[]{:S(2)}) collective-permute-start(bf16[2,160,640]{2,1,0:T(8,128)(2,1)S(1)} %pad_maximum_fusion.6.refs_9_), channel_id=1, source_target_pairs={{0,24},{1,25},{2,26},{3,27},{4,28},{5,29},{6,30},{7,31},{8,0},{9,1... | collective-permute-start | bytes 1228808 | tf_op jit(solution)/shard_map/ppermute | solution.py:37
  94.3 23.1 %collective-permute-start.14 = (bf16[2,160,640]{2,1,0:T(8,128)(2,1)S(1)}, bf16[2,160,640]{2,1,0:T(8,128)(2,1)S(1)}, u32[]{:S(2)}, u32[]{:S(2)}) collective-permute-start(bf16[2,160,640]{2,1,0:T(8,128)(2,1)S(1)} %pad_maximum_fusion.5.refs_12_), channel_id=1, source_target_pairs={{0,224},{1,225},{2,226},{3,227},{4,228},{5,229},{6,230},{7,231},{8... | collective-permute-start | bytes 1228808 | tf_op jit(solution)/shard_map/ppermute | solution.py:37
  108.2 16.8 %collective-permute-start.9 = (bf16[2,160,640]{2,1,0:T(8,128)(2,1)S(1)}, bf16[2,160,640]{2,1,0:T(8,128)(2,1)}, u32[]{:S(2)}, u32[]{:S(2)}) collective-permute-start(bf16[2,160,640]{2,1,0:T(8,128)(2,1)S(1)} %collective-permute-done.8.refs_6_), channel_id=1, source_target_pairs={{0,32},{1,33},{2,34},{3,35},{4,36},{5,37},{6,38},{7,39},{8,40},{9,... | collective-permute-start | bytes 1228808 | tf_op jit(solution)/shard_map/ppermute | solution.py:37
  117.4 19.0 %collective-permute-start.15 = (bf16[2,160,640]{2,1,0:T(8,128)(2,1)S(1)}, bf16[2,160,640]{2,1,0:T(8,128)(2,1)}, u32[]{:S(2)}, u32[]{:S(2)}) collective-permute-start(bf16[2,160,640]{2,1,0:T(8,128)(2,1)S(1)} %collective-permute-done.14.refs_14_), channel_id=1, source_target_pairs={{0,224},{1,225},{2,226},{3,227},{4,228},{5,229},{6,230},{7,231},{8... | collective-permute-start | bytes 1228808 | tf_op jit(solution)/shard_map/ppermute | solution.py:37
  119.7 16.9 %collective-permute-start.34 = (bf16[3,160,640]{2,1,0:T(8,128)(2,1)S(1)}, bf16[3,160,640]{2,1,0:T(8,128)(2,1)}, u32[]{:S(2)}, u32[]{:S(2)}) collective-permute-start(bf16[3,160,640]{2,1,0:T(8,128)(2,1)S(1)} %pad_maximum_fusion.2.refs_5_), channel_id=1, source_target_pairs={{0,8},{1,9},{2,10},{3,11},{4,12},{5,13},{6,14},{7,15},{8,16},{9,17... | collective-permute-start | bytes 1843208 | tf_op jit(solution)/shard_map/ppermute | solution.py:37
  125.0 17.9 %collective-permute-start.39 = (bf16[3,160,640]{2,1,0:T(8,128)(2,1)S(1)}, bf16[3,160,640]{2,1,0:T(8,128)(2,1)S(1)}, u32[]{:S(2)}, u32[]{:S(2)}) collective-permute-start(bf16[3,160,640]{2,1,0:T(8,128)(2,1)S(1)} %collective-permute-done.38.refs_7_), channel_id=1, source_target_pairs={{0,24},{1,25},{2,26},{3,27},{4,28},{5,29},{6,30},{7,31},{8,0},{9,1... | collective-permute-start | bytes 1843208 | tf_op jit(solution)/shard_map/ppermute | solution.py:37
  127.3 22.5 %collective-permute-start.35 = (bf16[3,160,640]{2,1,0:T(8,128)(2,1)S(1)}, bf16[3,160,640]{2,1,0:T(8,128)(2,1)S(1)}, u32[]{:S(2)}, u32[]{:S(2)}) collective-permute-start(bf16[3,160,640]{2,1,0:T(8,128)(2,1)S(1)} %pad_maximum_fusion.2.refs_5_), channel_id=1, source_target_pairs={{0,24},{1,25},{2,26},{3,27},{4,28},{5,29},{6,30},{7,31},{8,0},{9,1... | collective-permute-start | bytes 1843208 | tf_op jit(solution)/shard_map/ppermute | solution.py:37
  136.4 17.2 %collective-permute-start.3 = (bf16[512,640]{1,0:T(8,128)(2,1)S(1)}, bf16[512,640]{1,0:T(8,128)(2,1)S(1)}, u32[]{:S(2)}, u32[]{:S(2)}) collective-permute-start(bf16[512,640]{1,0:T(8,128)(2,1)S(1)} %attend.1.refs_1_.refs_2_), channel_id=1, source_target_pairs={{0,2},{1,3},{2,0},{3,1},{4,6},{5,7},{6,4},{7,5},{8,10},{9,11},{10,... | collective-permute-start | bytes 1966088 | tf_op jit(solution)/shard_map/ppermute | solution.py:37
  136.5 17.0 %collective-permute-start.10 = (bf16[2,160,640]{2,1,0:T(8,128)(2,1)}, bf16[2,160,640]{2,1,0:T(8,128)(2,1)}, u32[]{:S(2)}, u32[]{:S(2)}) collective-permute-start(bf16[2,160,640]{2,1,0:T(8,128)(2,1)} %collective-permute-done.9.refs_8_), channel_id=1, source_target_pairs={{0,32},{1,33},{2,34},{3,35},{4,36},{5,37},{6,38},{7,39},{8,40},{9,... | collective-permute-start | bytes 1228808 | tf_op jit(solution)/shard_map/ppermute | solution.py:37
  136.6 25.1 %collective-permute-start.36 = (bf16[3,160,640]{2,1,0:T(8,128)(2,1)}, bf16[3,160,640]{2,1,0:T(8,128)(2,1)}, u32[]{:S(2)}, u32[]{:S(2)}) collective-permute-start(bf16[3,160,640]{2,1,0:T(8,128)(2,1)} %collective-permute-done.34.refs_6_), channel_id=1, source_target_pairs={{0,8},{1,9},{2,10},{3,11},{4,12},{5,13},{6,14},{7,15},{8,16},{9,17... | collective-permute-start | bytes 1843208 | tf_op jit(solution)/shard_map/ppermute | solution.py:37
  153.5 32.1 %collective-permute-start.2 = (bf16[512,640]{1,0:T(8,128)(2,1)S(1)}, bf16[512,640]{1,0:T(8,128)(2,1)S(1)}, u32[]{:S(2)}, u32[]{:S(2)}) collective-permute-start(bf16[512,640]{1,0:T(8,128)(2,1)S(1)} %attend.1.refs_1_.refs_2_), channel_id=1, source_target_pairs={{0,1},{1,0},{2,3},{3,2},{4,5},{5,4},{6,7},{7,6},{8,9},{9,8},{10,11... | collective-permute-start | bytes 1966088 | tf_op jit(solution)/shard_map/ppermute | solution.py:37
  153.5 32.1 %collective-permute-start.4 = (bf16[512,640]{1,0:T(8,128)(2,1)S(1)}, bf16[512,640]{1,0:T(8,128)(2,1)S(1)}, u32[]{:S(2)}, u32[]{:S(2)}) collective-permute-start(bf16[512,640]{1,0:T(8,128)(2,1)S(1)} %collective-permute-done.3.refs_3_.refs_4_), channel_id=1, source_target_pairs={{0,1},{1,0},{2,3},{3,2},{4,5},{5,4},{6,7},{7,6},{8,9},{9,8},{10,11... | collective-permute-start | bytes 1966088 | tf_op jit(solution)/shard_map/ppermute | solution.py:37
  156.2 29.5 %collective-permute-start.23 = (bf16[2,160,640]{2,1,0:T(8,128)(2,1)}, bf16[2,160,640]{2,1,0:T(8,128)(2,1)}, u32[]{:S(2)}, u32[]{:S(2)}) collective-permute-start(bf16[2,160,640]{2,1,0:T(8,128)(2,1)} %copy-done.41), channel_id=1, source_target_pairs={{0,32},{1,33},{2,34},{3,35},{4,36},{5,37},{6,38},{7,39},{8,40},{9,... | collective-permute-start | bytes 1228808 | tf_op jit(solution)/shard_map/ppermute | solution.py:37
  161.7 35.1 %collective-permute-start.11 = (bf16[2,160,640]{2,1,0:T(8,128)(2,1)}, bf16[2,160,640]{2,1,0:T(8,128)(2,1)}, u32[]{:S(2)}, u32[]{:S(2)}) collective-permute-start(bf16[2,160,640]{2,1,0:T(8,128)(2,1)} %collective-permute-done.10.refs_10_), channel_id=1, source_target_pairs={{0,32},{1,33},{2,34},{3,35},{4,36},{5,37},{6,38},{7,39},{8,40},{9,... | collective-permute-start | bytes 1228808 | tf_op jit(solution)/shard_map/ppermute | solution.py:37
  161.7 35.1 %collective-permute-start.17 = (bf16[2,160,640]{2,1,0:T(8,128)(2,1)}, bf16[2,160,640]{2,1,0:T(8,128)(2,1)}, u32[]{:S(2)}, u32[]{:S(2)}) collective-permute-start(bf16[2,160,640]{2,1,0:T(8,128)(2,1)} %collective-permute-done.16.refs_18_), channel_id=1, source_target_pairs={{0,224},{1,225},{2,226},{3,227},{4,228},{5,229},{6,230},{7,231},{8... | collective-permute-start | bytes 1228808 | tf_op jit(solution)/shard_map/ppermute | solution.py:37
  (69 other events, 946.4 us)
where the time goes:
time: 202 us
  starting transfers between devices  76.4 us (38%)
  waiting for transfers between devices  70.1 us (35%)
  Pallas kernels  32.3 us (16%)
  local copies, waits for them, and re-layouts  19.4 us (10%)
    ppermute x41, starting transfers between devices, send(): return lax.ppermute(a, AXES, pairs(move))  72.6 us
    ppermute x41, waiting for transfers between devices, send(): return lax.ppermute(a, AXES, pairs(move))  70.1 us
    pallas_call x4, Pallas kernels, run(): pl.pallas_call(kernel, out_shape=out_shape, in_specs=specs, out_specs=out...  23.4 us
    unnamed x100, local copies, waits for them, and re-layouts  17.9 us
    pallas_call x1, Pallas kernels, body(): pl.pallas_call(attn_kernel, out_shape=jax.ShapeDtypeStruct((2 * tokens, w...  8.94 us
  transfers between devices with their start and end apart: 43, of which 15 were waited for; matrix products, arithmetic and copies ran while one was open for 1% of the time, Pallas kernels for 14%

commit v1 on v0

--- a/solution.py
+++ b/solution.py
@@ -170,21 +170,42 @@
 
 def mid_kernel(*refs):
     where = refs[0]
-    ats = refs[1:5]
-    za = refs[5:12]
-    zb = refs[12:19]
-    acc = refs[19]
-    wz, att, sem_z, sem_a = refs[20:]
-    heads = [pltpu.make_async_copy(ats[j], att.at[j], sem_a.at[j]) for j in range(4)]
+    ths = refs[1:5]
+    ats = refs[5:9]
+    rest = refs[9:13]
+    za = refs[13:20]
+    zb = refs[20:27]
+    before, acc, vel = refs[27:30]
+    wz, wy, att, tea, sem_z, sem_y, sem_a, sem_t = refs[30:]
+    lo, n = SPANS[2]
+    heads = [pltpu.make_async_copy(ths[j], tea.at[j], sem_t.at[j]) for j in range(4)]
     for c in heads:
+        c.start()
+    for j, dy in enumerate(YD):
+        dst = wy.at[pl.ds(0, n), rows_of(where, dy)]
+        pltpu.make_async_copy(rest[j], dst, sem_y.at[0]).start()
+    more = [pltpu.make_async_copy(ats[j], att.at[j], sem_a.at[j]) for j in range(4)]
+    for c in more:
         c.start()
     for i in range(7):
         for j, dy in enumerate(YD):
             buf = (za, zb)[j // 2][i]
             dst = wz.at[i, rows_of(where, dy)]
             pltpu.make_async_copy(buf.at[j % 2], dst, sem_z.at[i]).start()
+    vel[...] = before[...]
     acc[...] = jnp.zeros_like(acc)
     for c in heads:
+        c.wait()
+    pltpu.make_async_copy(wy, wy, sem_y.at[0]).wait()
+
+    def teach(k, carry):
+        kb = where[4 + lo + k]
+        hf = where[12 + lo + k]
+        vel[hf] += lax.dot_general(tea[kb], wy[k], NT_DIMS, preferred_element_type=jnp.float32)
+        return carry
+
+    lax.fori_loop(0, n, teach, 0)
+    for c in more:
         c.wait()
 
     def step(k, carry):
@@ -360,14 +381,14 @@
     full = jax.ShapeDtypeStruct((2, 2 * tokens, HALF), f32)
     half = jax.ShapeDtypeStruct((2, tokens, HALF), f32)
 
-    def run(kernel, out_shape, ins, specs, outs, scratch):
+    def run(kernel, out_shape, ins, specs, outs, scratch, grant=16):
         return pl.pallas_call(
             kernel,
             out_shape=out_shape,
             in_specs=specs,
             out_specs=outs,
             scratch_shapes=scratch,
-            compiler_params=pltpu.CompilerParams(vmem_limit_bytes=16 << 20),
+            compiler_params=pltpu.CompilerParams(vmem_limit_bytes=grant << 20),
         )(*ins)
 
     def teach(spans, bufs, *before):
@@ -387,19 +408,23 @@
         )
 
     vel = teach(SPANS[:CUT], sets[: 4 * CUT])
-    vel = teach(SPANS[CUT:], sets[4 * CUT :], vel)
-    acc = run(
+    acc, vel = run(
         mid_kernel,
-        full,
-        (where, *at, *za, *zb),
-        [sm] + [hb] * 18,
-        vm,
+        (full, half),
+        (where, *th, *at, *sets[8:], *za, *zb, vel),
+        [sm] + [hb] * 26 + [vm],
+        (vm, vm),
         [
             pltpu.VMEM((7, HALF, width), bf),
+            pltpu.VMEM((3, HALF, width), bf),
             pltpu.VMEM((4, 2 * tokens, width), bf),
+            pltpu.VMEM((4, tokens, width), bf),
             dma((7,)),
+            dma((1,)),
+            dma((4,)),
             dma((4,)),
         ],
+        19,
     )
     return run(
         last_kernel,

time: 202 us -> 208 us (1.030)
  the two profiles are of different devices: /device:TPU:28 before, /device:TPU:6 now
where the time goes in v1:
time: 208 us; the launch traced here: 207 us
  starting transfers between devices  94.5 us (45%)
  waiting for transfers between devices  55.2 us (27%)
  Pallas kernels  31.9 us (15%)
  local copies, waits for them, and re-layouts  22.3 us (11%)
    ppermute x41, starting transfers between devices, send(): return lax.ppermute(a, AXES, pairs(move))  86 us
    ppermute x41, waiting for transfers between devices, send(): return lax.ppermute(a, AXES, pairs(move))  55.2 us
    pallas_call x3, Pallas kernels, run(): pl.pallas_call(kernel, out_shape=out_shape, in_specs=specs, out_specs=out...  22.9 us
    unnamed x112, local copies, waits for them, and re-layouts  20.8 us
    pallas_call x1, Pallas kernels, body(): pl.pallas_call(attn_kernel, out_shape=jax.ShapeDtypeStruct((2 * tokens, w...  8.93 us
    ppermute x1, starting transfers between devices, body(): lax.ppermute(jnp.stack([a[tokens - REACH:] for a in arrays]), 'seq', fwd)  5.23 us
  transfers between devices with their start and end apart: 43, of which 13 were waited for; matrix products, arithmetic and copies ran while one was open for 1% of the time, Pallas kernels for 13%

profile of v1, /device:TPU:6, one launch (start us, length us, event | category | flops | bytes accessed | tf_op | source)
XLA Modules:
  0.0 207.3 jit_solution(6272324562855597966)
XLA Ops:
  1.6 8.5 %collective-permute-start.5 = (bf16[2,80,640]{2,1,0:T(8,128)(2,1)S(1)}, bf16[2,80,640]{2,1,0:T(8,128)(2,1)S(1)}, u32[]{:S(2)}, u32[]{:S(2)}) collective-permute-start(bf16[2,80,640]{2,1,0:T(8,128)(2,1)S(1)} %pad_maximum_fusion.8), channel_id=1, source_target_pairs={{0,0},{1,224},{2,192},{3,160},{4,4},{5,228},{6,196},{7,164},{8,8},... | collective-permute-start | bytes 614408 | tf_op jit(solution)/shard_map/ppermute | solution.py:37
  14.2 5.7 %collective-permute-done.5 = bf16[2,80,640]{2,1,0:T(8,128)(2,1)S(1)} collective-permute-done((bf16[2,80,640]{2,1,0:T(8,128)(2,1)S(1)}, bf16[2,80,640]{2,1,0:T(8,128)(2,1)S(1)}, u32[]{:S(2)}, u32[]{:S(2)}) %collective-permute-start.5) | collective-permute-done | bytes 204832 | tf_op jit(solution)/shard_map/ppermute | solution.py:37
  19.9 4.3 %collective-permute-done.6 = bf16[2,80,640]{2,1,0:T(8,128)(2,1)S(1)} collective-permute-done((bf16[2,80,640]{2,1,0:T(8,128)(2,1)S(1)}, bf16[2,80,640]{2,1,0:T(8,128)(2,1)S(1)}, u32[]{:S(2)}, u32[]{:S(2)}) %collective-permute-start.6) | collective-permute-done | bytes 204832 | tf_op jit(solution)/shard_map/ppermute | solution.py:37
  32.7 3.2 %collective-permute-start.1 = (bf16[4,192,640]{2,1,0:T(8,128)(2,1)S(1)}, bf16[4,192,640]{2,1,0:T(8,128)(2,1)S(1)}, u32[]{:S(2)}, u32[]{:S(2)}) collective-permute-start(bf16[4,192,640]{2,1,0:T(8,128)(2,1)S(1)} %pad_maximum_fusion.1), channel_id=1, source_target_pairs={{4,0},{8,4},{12,8},{16,12},{20,16},{24,20},{28,24},{32,28},{36,32}... | collective-permute-start | bytes 2949128 | tf_op jit(solution)/shard_map/ppermute | solution.py:301
  36.1 3.1 %collective-permute-start.25 = (bf16[160,640]{1,0:T(8,128)(2,1)S(1)}, bf16[160,640]{1,0:T(8,128)(2,1)S(1)}, u32[]{:S(2)}, u32[]{:S(2)}) collective-permute-start(bf16[160,640]{1,0:T(8,128)(2,1)S(1)} %collective-permute-done.24), channel_id=1, source_target_pairs={{0,224},{1,225},{2,226},{3,227},{4,228},{5,229},{6,230},{7,231},{8... | collective-permute-start | bytes 614408 | tf_op jit(solution)/shard_map/ppermute | solution.py:37
  40.9 5.2 %collective-permute-start = (bf16[4,192,640]{2,1,0:T(8,128)(2,1)S(1)}, bf16[4,192,640]{2,1,0:T(8,128)(2,1)S(1)}, u32[]{:S(2)}, u32[]{:S(2)}) collective-permute-start(bf16[4,192,640]{2,1,0:T(8,128)(2,1)S(1)} %pad_maximum_fusion), channel_id=1, source_target_pairs={{0,4},{4,8},{8,12},{12,16},{16,20},{20,24},{24,28},{28,32},{32,36}... | collective-permute-start | bytes 2949128 | tf_op jit(solution)/shard_map/ppermute | solution.py:300
  47.6 3.2 %collective-permute-start.26 = (bf16[160,640]{1,0:T(8,128)(2,1)S(1)}, bf16[160,640]{1,0:T(8,128)(2,1)S(1)}, u32[]{:S(2)}, u32[]{:S(2)}) collective-permute-start(bf16[160,640]{1,0:T(8,128)(2,1)S(1)} %collective-permute-done.25), channel_id=1, source_target_pairs={{0,224},{1,225},{2,226},{3,227},{4,228},{5,229},{6,230},{7,231},{8... | collective-permute-start | bytes 614408 | tf_op jit(solution)/shard_map/ppermute | solution.py:37
  50.9 12.0 %collective-permute-done.23 = bf16[160,640]{1,0:T(8,128)(2,1)S(1)} collective-permute-done((bf16[160,640]{1,0:T(8,128)(2,1)S(1)}, bf16[160,640]{1,0:T(8,128)(2,1)S(1)}, u32[]{:S(2)}, u32[]{:S(2)}) %collective-permute-start.23) | collective-permute-done | bytes 204832 | tf_op jit(solution)/shard_map/ppermute | solution.py:37
  63.2 21.3 %collective-permute-start.38 = (bf16[3,160,640]{2,1,0:T(8,128)(2,1)S(1)}, bf16[3,160,640]{2,1,0:T(8,128)(2,1)S(1)}, u32[]{:S(2)}, u32[]{:S(2)}) collective-permute-start(bf16[3,160,640]{2,1,0:T(8,128)(2,1)S(1)} %pad_maximum_fusion.3.refs_5_), channel_id=1, source_target_pairs={{0,24},{1,25},{2,26},{3,27},{4,28},{5,29},{6,30},{7,31},{8,0},{9,1... | collective-permute-start | bytes 1843208 | tf_op jit(solution)/shard_map/ppermute | solution.py:37
  84.7 8.3 %collective-permute-start.41 = (bf16[2,160,640]{2,1,0:T(8,128)(2,1)S(1)}, bf16[2,160,640]{2,1,0:T(8,128)(2,1)S(1)}, u32[]{:S(2)}, u32[]{:S(2)}) collective-permute-start(bf16[2,160,640]{2,1,0:T(8,128)(2,1)S(1)} %pad_maximum_fusion.6.refs_9_), channel_id=1, source_target_pairs={{0,24},{1,25},{2,26},{3,27},{4,28},{5,29},{6,30},{7,31},{8,0},{9,1... | collective-permute-start | bytes 1228808 | tf_op jit(solution)/shard_map/ppermute | solution.py:37
  93.2 3.2 %collective-permute-start.14 = (bf16[2,160,640]{2,1,0:T(8,128)(2,1)S(1)}, bf16[2,160,640]{2,1,0:T(8,128)(2,1)S(1)}, u32[]{:S(2)}, u32[]{:S(2)}) collective-permute-start(bf16[2,160,640]{2,1,0:T(8,128)(2,1)S(1)} %pad_maximum_fusion.5.refs_20_), channel_id=1, source_target_pairs={{0,224},{1,225},{2,226},{3,227},{4,228},{5,229},{6,230},{7,231},{8... | collective-permute-start | bytes 1228808 | tf_op jit(solution)/shard_map/ppermute | solution.py:37
  103.3 5.7 %collective-permute-done.40.refs_10_ = bf16[2,160,640]{2,1,0:T(8,128)(2,1)S(1)} collective-permute-done((bf16[2,160,640]{2,1,0:T(8,128)(2,1)S(1)}, bf16[2,160,640]{2,1,0:T(8,128)(2,1)S(1)}, u32[]{:S(2)}, u32[]{:S(2)}) %collective-permute-start.40) | collective-permute-done | bytes 409632 | tf_op jit(solution)/shard_map/ppermute | solution.py:37
  109.8 3.2 %collective-permute-start.32 = (bf16[2,160,640]{2,1,0:T(8,128)(2,1)S(1)}, bf16[2,160,640]{2,1,0:T(8,128)(2,1)}, u32[]{:S(2)}, u32[]{:S(2)}) collective-permute-start(bf16[2,160,640]{2,1,0:T(8,128)(2,1)S(1)} %collective-permute-done.31.refs_15_), channel_id=1, source_target_pairs={{0,224},{1,225},{2,226},{3,227},{4,228},{5,229},{6,230},{7,231},{8... | collective-permute-start | bytes 1228808 | tf_op jit(solution)/shard_map/ppermute | solution.py:37
  114.7 6.8 %collective-permute-start.39 = (bf16[3,160,640]{2,1,0:T(8,128)(2,1)S(1)}, bf16[3,160,640]{2,1,0:T(8,128)(2,1)S(1)}, u32[]{:S(2)}, u32[]{:S(2)}) collective-permute-start(bf16[3,160,640]{2,1,0:T(8,128)(2,1)S(1)} %collective-permute-done.38.refs_7_), channel_id=1, source_target_pairs={{0,24},{1,25},{2,26},{3,27},{4,28},{5,29},{6,30},{7,31},{8,0},{9,1... | collective-permute-start | bytes 1843208 | tf_op jit(solution)/shard_map/ppermute | solution.py:37
  128.8 4.2 %collective-permute-start.29 = (bf16[3,160,640]{2,1,0:T(8,128)(2,1)S(1)}, bf16[3,160,640]{2,1,0:T(8,128)(2,1)S(1)}, u32[]{:S(2)}, u32[]{:S(2)}) collective-permute-start(bf16[3,160,640]{2,1,0:T(8,128)(2,1)S(1)} %pad_maximum_fusion.2.refs_9_), channel_id=1, source_target_pairs={{0,24},{1,25},{2,26},{3,27},{4,28},{5,29},{6,30},{7,31},{8,0},{9,1... | collective-permute-start | bytes 1843208 | tf_op jit(solution)/shard_map/ppermute | solution.py:37
  133.1 8.9 %attend.1.refs_5_.refs_2_ = bf16[512,640]{1,0:T(8,128)(2,1)S(1)} custom-call(s32[2]{0:T(128)S(1)} %pad_add_fusion.where, s32[4]{0:T(128)S(1)} %copy-done.53, bf16[256,640]{1,0:T(8,128)(2,1)S(1)} %copy-done.51, bf16[256,640]{1,0:T(8,128)(2,1)S(1)} %copy-done.52, bf16[256,640]{1,0:T(8,128)(2,1)S(1)} %copy-done.2, bf16[256,640]{1,0:T(8,128)(2,1)S(1)} %copy-done.3, ...), custom_call_target="tpu_custom_call" | custom-call | tf_op jit(solution)/shard_map/attend/pallas_call | solution.py:355
  142.1 3.7 %collective-permute-start.3 = (bf16[512,640]{1,0:T(8,128)(2,1)S(1)}, bf16[512,640]{1,0:T(8,128)(2,1)S(1)}, u32[]{:S(2)}, u32[]{:S(2)}) collective-permute-start(bf16[512,640]{1,0:T(8,128)(2,1)S(1)} %attend.1.refs_5_.refs_2_), channel_id=1, source_target_pairs={{0,2},{1,3},{2,0},{3,1},{4,6},{5,7},{6,4},{7,5},{8,10},{9,11},{10,... | collective-permute-start | bytes 1966088 | tf_op jit(solution)/shard_map/ppermute | solution.py:37
  147.4 3.2 %collective-permute-start.33 = (bf16[2,160,640]{2,1,0:T(8,128)(2,1)}, bf16[2,160,640]{2,1,0:T(8,128)(2,1)}, u32[]{:S(2)}, u32[]{:S(2)}) collective-permute-start(bf16[2,160,640]{2,1,0:T(8,128)(2,1)} %collective-permute-done.32.refs_17_), channel_id=1, source_target_pairs={{0,224},{1,225},{2,226},{3,227},{4,228},{5,229},{6,230},{7,231},{8... | collective-permute-start | bytes 1228808 | tf_op jit(solution)/shard_map/ppermute | solution.py:37
  151.5 8.2 %collective-permute-done.10.refs_18_ = bf16[2,160,640]{2,1,0:T(8,128)(2,1)S(1)} collective-permute-done((bf16[2,160,640]{2,1,0:T(8,128)(2,1)S(1)}, bf16[2,160,640]{2,1,0:T(8,128)(2,1)S(1)}, u32[]{:S(2)}, u32[]{:S(2)}) %collective-permute-start.10) | collective-permute-done | bytes 409632 | tf_op jit(solution)/shard_map/ppermute | solution.py:37
  160.8 8.0 %collective-permute-done.16.refs_26_ = bf16[2,160,640]{2,1,0:T(8,128)(2,1)} collective-permute-done((bf16[2,160,640]{2,1,0:T(8,128)(2,1)}, bf16[2,160,640]{2,1,0:T(8,128)(2,1)}, u32[]{:S(2)}, u32[]{:S(2)}) %collective-permute-start.16) | collective-permute-done | bytes 409632 | tf_op jit(solution)/shard_map/ppermute | solution.py:37
  168.8 3.7 %collective-permute-start.17 = (bf16[2,160,640]{2,1,0:T(8,128)(2,1)}, bf16[2,160,640]{2,1,0:T(8,128)(2,1)}, u32[]{:S(2)}, u32[]{:S(2)}) collective-permute-start(bf16[2,160,640]{2,1,0:T(8,128)(2,1)} %collective-permute-done.16.refs_26_), channel_id=1, source_target_pairs={{0,224},{1,225},{2,226},{3,227},{4,228},{5,229},{6,230},{7,231},{8... | collective-permute-start | bytes 1228808 | tf_op jit(solution)/shard_map/ppermute | solution.py:37
  183.9 4.1 %shard_map.149.refs_27_ = f32[2,256,640]{2,1,0:T(8,128)S(1)} custom-call(s32[20]{0:T(128)S(1)} %concatenate.6.refs_0_, bf16[256,640]{1,0:T(8,128)(2,1)S(1)} %copy-done.12, bf16[256,640]{1,0:T(8,128)(2,1)S(1)} %copy-done.18, bf16[256,640]{1,0:T(8,128)(2,1)S(1)} %copy-done.15, bf16[256,640]{1,0:T(8,128)(2,1)S(1)} %copy-done.21, ...), custom_call_target="tpu_custom_call" | custom-call | tf_op jit(solution)/shard_map/pallas_call | solution.py:385
  188.3 14.3 %shard_map.150 = (f32[2,512,640]{2,1,0:T(8,128)S(1)}, f32[2,256,640]{2,1,0:T(8,128)S(1)}) custom-call(s32[20]{0:T(128)S(1)} %concatenate.6.refs_0_, bf16[256,640]{1,0:T(8,128)(2,1)S(1)} %copy-done.13, bf16[256,640]{1,0:T(8,128)(2,1)S(1)} %copy-done.19, bf16[256,640]{1,0:T(8,128)(2,1)S(1)} %copy-done.16, bf16[256,640]{1,0:T(8,128)(2,1)S(1)} %copy-done.22, ...), custom_call_target="tpu_custom_call" | custom-call | tf_op jit(solution)/shard_map/pallas_call | solution.py:385
  202.6 4.6 %shard_map.151 = (f32[256,1280]{1,0:T(8,128)}, f32[256,1280]{1,0:T(8,128)}) custom-call(s32[20]{0:T(128)S(1)} %concatenate.6.refs_0_, f32[2,4]{1,0:T(2,128)S(1)} %pad_maximum_fusion.9.refs_1_, bf16[512,640]{1,0:T(8,128)(2,1)S(1)} %attend.1.refs_5_.refs_2_, bf16[512,640]{1,0:T(8,128)(2,1)S(1)} %collective-permute-done.2.refs_6_.refs_3_, ...), custom_call_target="tpu_custom_call" | custom-call | tf_op jit(solution)/shard_map/pallas_call | solution.py:385
  (196 shorter events, 49.0 us)
Async XLA Ops:
  1.6 18.3 %collective-permute-start.5 = (bf16[2,80,640]{2,1,0:T(8,128)(2,1)S(1)}, bf16[2,80,640]{2,1,0:T(8,128)(2,1)S(1)}, u32[]{:S(2)}, u32[]{:S(2)}) collective-permute-start(bf16[2,80,640]{2,1,0:T(8,128)(2,1)S(1)} %pad_maximum_fusion.8), channel_id=1, source_target_pairs={{0,0},{1,224},{2,192},{3,160},{4,4},{5,228},{6,196},{7,164},{8,8},... | collective-permute-start | bytes 614408 | tf_op jit(solution)/shard_map/ppermute | solution.py:37
  11.2 18.0 %collective-permute-start.19 = (bf16[256,640]{1,0:T(8,128)(2,1)}, bf16[256,640]{1,0:T(8,128)(2,1)S(1)}, u32[]{:S(2)}, u32[]{:S(2)}) collective-permute-start(bf16[256,640]{1,0:T(8,128)(2,1)} %refs_1_.3), channel_id=1, source_target_pairs={{0,2},{1,3},{2,0},{3,1},{4,6},{5,7},{6,4},{7,5},{8,10},{9,11},{10,... | collective-permute-start | bytes 983048 | tf_op jit(solution)/shard_map/ppermute | solution.py:37
  11.2 21.5 %collective-permute-start.18 = (bf16[256,640]{1,0:T(8,128)(2,1)}, bf16[256,640]{1,0:T(8,128)(2,1)S(1)}, u32[]{:S(2)}, u32[]{:S(2)}) collective-permute-start(bf16[256,640]{1,0:T(8,128)(2,1)} %refs_1_.3), channel_id=1, source_target_pairs={{0,1},{1,0},{2,3},{3,2},{4,5},{5,4},{6,7},{7,6},{8,9},{9,8},{10,11... | collective-permute-start | bytes 983048 | tf_op jit(solution)/shard_map/ppermute | solution.py:37
  32.7 52.0 %collective-permute-start.1 = (bf16[4,192,640]{2,1,0:T(8,128)(2,1)S(1)}, bf16[4,192,640]{2,1,0:T(8,128)(2,1)S(1)}, u32[]{:S(2)}, u32[]{:S(2)}) collective-permute-start(bf16[4,192,640]{2,1,0:T(8,128)(2,1)S(1)} %pad_maximum_fusion.1), channel_id=1, source_target_pairs={{4,0},{8,4},{12,8},{16,12},{20,16},{24,20},{28,24},{32,28},{36,32}... | collective-permute-start | bytes 2949128 | tf_op jit(solution)/shard_map/ppermute | solution.py:301
  40.9 52.2 %collective-permute-start = (bf16[4,192,640]{2,1,0:T(8,128)(2,1)S(1)}, bf16[4,192,640]{2,1,0:T(8,128)(2,1)S(1)}, u32[]{:S(2)}, u32[]{:S(2)}) collective-permute-start(bf16[4,192,640]{2,1,0:T(8,128)(2,1)S(1)} %pad_maximum_fusion), channel_id=1, source_target_pairs={{0,4},{4,8},{8,12},{12,16},{16,20},{20,24},{24,28},{28,32},{32,36}... | collective-permute-start | bytes 2949128 | tf_op jit(solution)/shard_map/ppermute | solution.py:300
  46.2 38.3 %collective-permute-start.8 = (bf16[2,160,640]{2,1,0:T(8,128)(2,1)S(1)}, bf16[2,160,640]{2,1,0:T(8,128)(2,1)S(1)}, u32[]{:S(2)}, u32[]{:S(2)}) collective-permute-start(bf16[2,160,640]{2,1,0:T(8,128)(2,1)S(1)} %pad_maximum_fusion.4.refs_13_), channel_id=1, source_target_pairs={{0,32},{1,33},{2,34},{3,35},{4,36},{5,37},{6,38},{7,39},{8,40},{9,... | collective-permute-start | bytes 1228808 | tf_op jit(solution)/shard_map/ppermute | solution.py:37
  62.9 21.8 %collective-permute-start.31 = (bf16[2,160,640]{2,1,0:T(8,128)(2,1)S(1)}, bf16[2,160,640]{2,1,0:T(8,128)(2,1)S(1)}, u32[]{:S(2)}, u32[]{:S(2)}) collective-permute-start(bf16[2,160,640]{2,1,0:T(8,128)(2,1)S(1)} %pad_maximum_fusion.4.refs_13_), channel_id=1, source_target_pairs={{0,224},{1,225},{2,226},{3,227},{4,228},{5,229},{6,230},{7,231},{8... | collective-permute-start | bytes 1228808 | tf_op jit(solution)/shard_map/ppermute | solution.py:37
  63.2 35.5 %collective-permute-start.38 = (bf16[3,160,640]{2,1,0:T(8,128)(2,1)S(1)}, bf16[3,160,640]{2,1,0:T(8,128)(2,1)S(1)}, u32[]{:S(2)}, u32[]{:S(2)}) collective-permute-start(bf16[3,160,640]{2,1,0:T(8,128)(2,1)S(1)} %pad_maximum_fusion.3.refs_5_), channel_id=1, source_target_pairs={{0,24},{1,25},{2,26},{3,27},{4,28},{5,29},{6,30},{7,31},{8,0},{9,1... | collective-permute-start | bytes 1843208 | tf_op jit(solution)/shard_map/ppermute | solution.py:37
  84.5 17.9 %collective-permute-start.37 = (bf16[3,160,640]{2,1,0:T(8,128)(2,1)S(1)}, bf16[3,160,640]{2,1,0:T(8,128)(2,1)S(1)}, u32[]{:S(2)}, u32[]{:S(2)}) collective-permute-start(bf16[3,160,640]{2,1,0:T(8,128)(2,1)S(1)} %pad_maximum_fusion.3.refs_5_), channel_id=1, source_target_pairs={{0,8},{1,9},{2,10},{3,11},{4,12},{5,13},{6,14},{7,15},{8,16},{9,17... | collective-permute-start | bytes 1843208 | tf_op jit(solution)/shard_map/ppermute | solution.py:37
  84.6 24.3 %collective-permute-start.40 = (bf16[2,160,640]{2,1,0:T(8,128)(2,1)S(1)}, bf16[2,160,640]{2,1,0:T(8,128)(2,1)S(1)}, u32[]{:S(2)}, u32[]{:S(2)}) collective-permute-start(bf16[2,160,640]{2,1,0:T(8,128)(2,1)S(1)} %pad_maximum_fusion.6.refs_9_), channel_id=1, source_target_pairs={{0,8},{1,9},{2,10},{3,11},{4,12},{5,13},{6,14},{7,15},{8,16},{9,17... | collective-permute-start | bytes 1228808 | tf_op jit(solution)/shard_map/ppermute | solution.py:37
  84.7 24.3 %collective-permute-start.41 = (bf16[2,160,640]{2,1,0:T(8,128)(2,1)S(1)}, bf16[2,160,640]{2,1,0:T(8,128)(2,1)S(1)}, u32[]{:S(2)}, u32[]{:S(2)}) collective-permute-start(bf16[2,160,640]{2,1,0:T(8,128)(2,1)S(1)} %pad_maximum_fusion.6.refs_9_), channel_id=1, source_target_pairs={{0,24},{1,25},{2,26},{3,27},{4,28},{5,29},{6,30},{7,31},{8,0},{9,1... | collective-permute-start | bytes 1228808 | tf_op jit(solution)/shard_map/ppermute | solution.py:37
  93.2 20.7 %collective-permute-start.14 = (bf16[2,160,640]{2,1,0:T(8,128)(2,1)S(1)}, bf16[2,160,640]{2,1,0:T(8,128)(2,1)S(1)}, u32[]{:S(2)}, u32[]{:S(2)}) collective-permute-start(bf16[2,160,640]{2,1,0:T(8,128)(2,1)S(1)} %pad_maximum_fusion.5.refs_20_), channel_id=1, source_target_pairs={{0,224},{1,225},{2,226},{3,227},{4,228},{5,229},{6,230},{7,231},{8... | collective-permute-start | bytes 1228808 | tf_op jit(solution)/shard_map/ppermute | solution.py:37
  113.9 28.3 %collective-permute-start.15 = (bf16[2,160,640]{2,1,0:T(8,128)(2,1)S(1)}, bf16[2,160,640]{2,1,0:T(8,128)(2,1)}, u32[]{:S(2)}, u32[]{:S(2)}) collective-permute-start(bf16[2,160,640]{2,1,0:T(8,128)(2,1)S(1)} %collective-permute-done.14.refs_22_), channel_id=1, source_target_pairs={{0,224},{1,225},{2,226},{3,227},{4,228},{5,229},{6,230},{7,231},{8... | collective-permute-start | bytes 1228808 | tf_op jit(solution)/shard_map/ppermute | solution.py:37
  114.7 31.1 %collective-permute-start.39 = (bf16[3,160,640]{2,1,0:T(8,128)(2,1)S(1)}, bf16[3,160,640]{2,1,0:T(8,128)(2,1)S(1)}, u32[]{:S(2)}, u32[]{:S(2)}) collective-permute-start(bf16[3,160,640]{2,1,0:T(8,128)(2,1)S(1)} %collective-permute-done.38.refs_7_), channel_id=1, source_target_pairs={{0,24},{1,25},{2,26},{3,27},{4,28},{5,29},{6,30},{7,31},{8,0},{9,1... | collective-permute-start | bytes 1843208 | tf_op jit(solution)/shard_map/ppermute | solution.py:37
  122.3 23.5 %collective-permute-start.35 = (bf16[2,160,640]{2,1,0:T(8,128)(2,1)S(1)}, bf16[2,160,640]{2,1,0:T(8,128)(2,1)}, u32[]{:S(2)}, u32[]{:S(2)}) collective-permute-start(bf16[2,160,640]{2,1,0:T(8,128)(2,1)S(1)} %collective-permute-done.34.refs_21_), channel_id=1, source_target_pairs={{0,32},{1,33},{2,34},{3,35},{4,36},{5,37},{6,38},{7,39},{8,40},{9,... | collective-permute-start | bytes 1228808 | tf_op jit(solution)/shard_map/ppermute | solution.py:37
  125.3 22.1 %collective-permute-start.28 = (bf16[3,160,640]{2,1,0:T(8,128)(2,1)S(1)}, bf16[3,160,640]{2,1,0:T(8,128)(2,1)}, u32[]{:S(2)}, u32[]{:S(2)}) collective-permute-start(bf16[3,160,640]{2,1,0:T(8,128)(2,1)S(1)} %pad_maximum_fusion.2.refs_9_), channel_id=1, source_target_pairs={{0,8},{1,9},{2,10},{3,11},{4,12},{5,13},{6,14},{7,15},{8,16},{9,17... | collective-permute-start | bytes 1843208 | tf_op jit(solution)/shard_map/ppermute | solution.py:37
  128.8 21.9 %collective-permute-start.29 = (bf16[3,160,640]{2,1,0:T(8,128)(2,1)S(1)}, bf16[3,160,640]{2,1,0:T(8,128)(2,1)S(1)}, u32[]{:S(2)}, u32[]{:S(2)}) collective-permute-start(bf16[3,160,640]{2,1,0:T(8,128)(2,1)S(1)} %pad_maximum_fusion.2.refs_9_), channel_id=1, source_target_pairs={{0,24},{1,25},{2,26},{3,27},{4,28},{5,29},{6,30},{7,31},{8,0},{9,1... | collective-permute-start | bytes 1843208 | tf_op jit(solution)/shard_map/ppermute | solution.py:37
  142.1 18.4 %collective-permute-start.3 = (bf16[512,640]{1,0:T(8,128)(2,1)S(1)}, bf16[512,640]{1,0:T(8,128)(2,1)S(1)}, u32[]{:S(2)}, u32[]{:S(2)}) collective-permute-start(bf16[512,640]{1,0:T(8,128)(2,1)S(1)} %attend.1.refs_5_.refs_2_), channel_id=1, source_target_pairs={{0,2},{1,3},{2,0},{3,1},{4,6},{5,7},{6,4},{7,5},{8,10},{9,11},{10,... | collective-permute-start | bytes 1966088 | tf_op jit(solution)/shard_map/ppermute | solution.py:37
  151.5 17.4 %collective-permute-start.16 = (bf16[2,160,640]{2,1,0:T(8,128)(2,1)}, bf16[2,160,640]{2,1,0:T(8,128)(2,1)}, u32[]{:S(2)}, u32[]{:S(2)}) collective-permute-start(bf16[2,160,640]{2,1,0:T(8,128)(2,1)} %collective-permute-done.15.refs_24_), channel_id=1, source_target_pairs={{0,224},{1,225},{2,226},{3,227},{4,228},{5,229},{6,230},{7,231},{8... | collective-permute-start | bytes 1228808 | tf_op jit(solution)/shard_map/ppermute | solution.py:37
  159.7 28.4 %collective-permute-start.30 = (bf16[3,160,640]{2,1,0:T(8,128)(2,1)}, bf16[3,160,640]{2,1,0:T(8,128)(2,1)}, u32[]{:S(2)}, u32[]{:S(2)}) collective-permute-start(bf16[3,160,640]{2,1,0:T(8,128)(2,1)} %collective-permute-done.28.refs_10_), channel_id=1, source_target_pairs={{0,8},{1,9},{2,10},{3,11},{4,12},{5,13},{6,14},{7,15},{8,16},{9,17... | collective-permute-start | bytes 1843208 | tf_op jit(solution)/shard_map/ppermute | solution.py:37
  160.5 27.6 %collective-permute-start.4 = (bf16[512,640]{1,0:T(8,128)(2,1)S(1)}, bf16[512,640]{1,0:T(8,128)(2,1)S(1)}, u32[]{:S(2)}, u32[]{:S(2)}) collective-permute-start(bf16[512,640]{1,0:T(8,128)(2,1)S(1)} %collective-permute-done.3.refs_7_.refs_4_), channel_id=1, source_target_pairs={{0,1},{1,0},{2,3},{3,2},{4,5},{5,4},{6,7},{7,6},{8,9},{9,8},{10,11... | collective-permute-start | bytes 1966088 | tf_op jit(solution)/shard_map/ppermute | solution.py:37
  160.8 27.3 %collective-permute-start.36 = (bf16[2,160,640]{2,1,0:T(8,128)(2,1)}, bf16[2,160,640]{2,1,0:T(8,128)(2,1)}, u32[]{:S(2)}, u32[]{:S(2)}) collective-permute-start(bf16[2,160,640]{2,1,0:T(8,128)(2,1)} %collective-permute-done.35.refs_23_), channel_id=1, source_target_pairs={{0,32},{1,33},{2,34},{3,35},{4,36},{5,37},{6,38},{7,39},{8,40},{9,... | collective-permute-start | bytes 1228808 | tf_op jit(solution)/shard_map/ppermute | solution.py:37
  160.8 41.7 %collective-permute-start.11 = (bf16[2,160,640]{2,1,0:T(8,128)(2,1)}, bf16[2,160,640]{2,1,0:T(8,128)(2,1)}, u32[]{:S(2)}, u32[]{:S(2)}) collective-permute-start(bf16[2,160,640]{2,1,0:T(8,128)(2,1)} %copy-done.49), channel_id=1, source_target_pairs={{0,32},{1,33},{2,34},{3,35},{4,36},{5,37},{6,38},{7,39},{8,40},{9,... | collective-permute-start | bytes 1228808 | tf_op jit(solution)/shard_map/ppermute | solution.py:37
  168.8 33.7 %collective-permute-start.17 = (bf16[2,160,640]{2,1,0:T(8,128)(2,1)}, bf16[2,160,640]{2,1,0:T(8,128)(2,1)}, u32[]{:S(2)}, u32[]{:S(2)}) collective-permute-start(bf16[2,160,640]{2,1,0:T(8,128)(2,1)} %collective-permute-done.16.refs_26_), channel_id=1, source_target_pairs={{0,224},{1,225},{2,226},{3,227},{4,228},{5,229},{6,230},{7,231},{8... | collective-permute-start | bytes 1228808 | tf_op jit(solution)/shard_map/ppermute | solution.py:37
  (75 other events, 961.6 us)
